TPU v7x, 32 devices: a whole 2x2x4 slice. The times are simulated.
32 devices in a mesh: wide: 16 (over z, y, x), narrow: 2 (over core).
Axes of the slice: x: 2, y: 2, z: 4, core: 2. Of those that a mesh axis runs over, the one named last changes fastest.
Arguments:
- samples: float32 [128, 32768], P('narrow', 'wide'), may hold values from -6 to 6
- row_weights: float32 [4096], P('narrow'), may hold values from 0.1 to 10
- tile_ranks: int32 [8, 64], P('narrow', 'wide'), may hold values from 16 to 80, as said below
- u_factors: bfloat16 [8, 64, 80, 512], P('narrow', 'wide'), may hold values from -0.125 to 0.125
- v_factors: bfloat16 [8, 64, 80, 512], P('narrow', 'wide'), may hold values from -0.25 to 0.25
Outputs:
- forward_rows: float32 [128, 4096], P('wide', 'narrow')
- adjoint_cols: float32 [128, 32768], P(None, ('wide', 'narrow'))
Inputs may be any that keep to these rules, and one draw needn't show every extreme that they name: `tile_ranks`: every rank is a multiple of 16.
All inputs are finite; a program needn't handle non-finite values.
Results may differ from a plain program's by a relative error of at most 0.0085.
Values may be sent and summed in bfloat16 or wider, within the bound.
A program may use at most 64 MiB of HBM per device.

v0:
```python
import jax
import jax.numpy as jnp
from jax import lax
from jax.sharding import PartitionSpec as P


def on_device(samples, row_weights, tile_ranks, u_factors, v_factors):
    tile_rows, tile_cols, rank_cap, tile_size = v_factors.shape
    columns = lax.all_gather(samples.astype(jnp.bfloat16), "narrow", axis=0, tiled=True)
    col_count = columns.shape[0]
    share_count = col_count // lax.axis_size("wide")
    columns = columns.reshape(col_count, tile_cols, tile_size)
    levels = lax.broadcasted_iota(jnp.int32, (1, 1, rank_cap), 2)
    rank_mask = (levels < tile_ranks[:, :, None]).astype(jnp.float32)[:, :, :, None]
    coeffs = jnp.einsum("sjb,ijrb->ijrs", columns, v_factors, preferred_element_type=jnp.float32)
    coeffs = (coeffs * rank_mask).astype(jnp.bfloat16)
    partial_value = jnp.einsum(
        "ijrs,ijrb->sib", coeffs, u_factors, preferred_element_type=jnp.float32
    )
    partial_value = partial_value.reshape(col_count, tile_rows * tile_size)
    row_total = lax.psum(partial_value, "wide")
    weighted = (row_total * row_weights[None, :]).astype(jnp.bfloat16)
    forward_rows = lax.dynamic_slice_in_dim(
        row_total, lax.axis_index("wide") * share_count, share_count, 0
    )
    weighted = weighted.reshape(col_count, tile_rows, tile_size)
    adjoint_coeffs = jnp.einsum(
        "sib,ijrb->ijrs", weighted, u_factors, preferred_element_type=jnp.float32
    )
    adjoint_coeffs = (adjoint_coeffs * rank_mask).astype(jnp.bfloat16)
    back = jnp.einsum(
        "ijrs,ijrb->sjb", adjoint_coeffs, v_factors, preferred_element_type=jnp.float32
    )
    back = back.reshape(col_count, tile_cols * tile_size)
    adjoint_cols = lax.psum_scatter(back, "narrow", scatter_dimension=1, tiled=True)
    return (forward_rows, adjoint_cols)


def solution(mesh):
    in_specs = (
        P("narrow", "wide"),
        P("narrow"),
        P("narrow", "wide"),
        P("narrow", "wide", None, None),
        P("narrow", "wide", None, None),
    )
    out_specs = (P("wide", "narrow"), P(None, ("wide", "narrow")))
    return jax.shard_map(
        on_device, mesh=mesh, in_specs=in_specs, out_specs=out_specs, check_vma=False
    )
```

profile of v0, /device:TPU:0, one launch (start us, length us, event | category | flops | bytes accessed | tf_op | source)
XLA Modules:
  0.0 153.5 jit_solution(15098324208993449909)
XLA Ops:
  7.2 0.0 copy-start
  7.2 0.0 all-reduce.2.cloned.1.call-start
  7.2 0.9 copy.10
  8.1 0.1 fusion.18
  8.2 1.1 convert_element_type.22
  9.2 2.3 %all_gather.3 = bf16[128,2048]{1,0:T(8,128)(2,1)S(1)} all-gather(bf16[64,2048]{1,0:T(8,128)(2,1)S(1)} %convert_element_type.22), channel_id=1, replica_groups=mesh['wide'=16,'narrow'=2] {'narrow'}, dimensions={0}, use_global_device_ids=true | all-gather | bytes 786432 | tf_op jit(solution)/shard_map/all_gather | solution.py:9
  11.5 0.3 copy.21
  11.8 0.0 copy-done
  11.8 2.3 %convolution_bitcast_fusion.1 = f32[128,4,512]{2,0,1:T(8,128)S(1)} fusion(bf16[4,4,80,512]{3,2,1,0:T(8,128)(2,1)S(1)} %copy-done, bf16[4,4,80,512]{3,2,1,0:T(8,128)(2,1)} %param.9, bf16[128,4,512,1]{0,2,1,3:T(8,128)(2,1)S(1)} %bitcast.34, f32[4,4,80]{2,1,0:T(4,128)S(1)} %copy.11), kind=kOutput, calls=%fused_computation.1 | convolution fusion | flops 335872000 | bytes 4199424 | tf_op jit(solution)/shard_map/ijrs,ijrb->sib/dot_general | solution.py:17
  14.1 0.0 copy-start.3
  14.1 1.3 copy.12
  15.5 0.0 copy-start.2
  15.5 0.0 all-reduce.2.cloned.1.call-update
  15.5 0.0 reduce-scatter.2.cloned.1.call-start
  15.6 115.2 %all-reduce.2.cloned.1.call-done = f32[128,2048]{0,1:T(8,128)} async-done(((f32[128,2048]{0,1:T(8,128)}), f32[128,2048]{0,1:T(8,128)}) %all-reduce.2.cloned.1.call-update) | async-done | bytes 1048592 | tf_op jit(solution)/shard_map/psum | solution.py:21
  130.7 0.0 copy-done.3
  130.8 1.6 %multiply_convert_fusion = bf16[128,2048]{0,1:T(8,128)(2,1)S(1)} fusion(f32[128,2048]{0,1:T(8,128)} %all-reduce.2.cloned.1.call-done, f32[2048]{0:T(1024)S(1)} %copy-done.3), kind=kLoop, calls=%fused_computation.11 | loop fusion | flops 524288 | bytes 1581056 | tf_op jit(solution)/shard_map/convert_element_type | solution.py:22
  132.3 0.0 copy-done.2
  132.3 2.0 %convolution_bitcast_fusion = f32[128,4,512]{2,0,1:T(8,128)} fusion(bf16[4,4,80,512]{3,2,1,0:T(8,128)(2,1)S(1)} %copy-done.2, bf16[128,4,512,1]{0,2,1,3:T(8,128)(2,1)S(1)} %bitcast.35, bf16[4,4,80,512]{3,2,1,0:T(8,128)(2,1)S(1)} %copy-done, f32[4,4,80]{2,0,1:T(4,128)S(1)} %fusion.18), kind=kOutput, calls=%fused_computation | convolution fusion | flops 335872000 | bytes 4199424 | tf_op jit(solution)/shard_map/ijrs,ijrb->sjb/dot_general | solution.py:31
  134.3 0.0 copy-start.1
  134.3 2.7 %copy.14 = f32[128,4,512]{0,2,1:T(8,128)} copy(f32[128,4,512]{2,0,1:T(8,128)} %convolution_bitcast_fusion) | data formatting | bytes 2097152 | tf_op jit(solution)/shard_map/ijrs,ijrb->sjb/transpose | solution.py:31
  137.0 0.0 reduce-scatter.2.cloned.1.call-update
  137.0 0.0 copy-done.1
  137.0 0.3 constant_dynamic-slice_fusion
  137.3 0.9 copy.15
  138.3 6.3 %reduce-scatter.2.cloned.1.call-done = f32[128,1024]{0,1:T(8,128)} async-done(((f32[128,2048]{0,1:T(8,128)}), f32[128,1024]{0,1:T(8,128)}) %reduce-scatter.2.cloned.1.call-update) | async-done | bytes 524304 | tf_op jit(solution)/shard_map/reduce_scatter | solution.py:35
  144.6 2.0 %copy.16 = f32[128,1024]{1,0:T(8,128)} copy(f32[128,1024]{0,1:T(8,128)} %reduce-scatter.2.cloned.1.call-done) | data formatting | bytes 1048576
  (1 shorter events, 0.0 us)
Async XLA Ops:
  7.2 4.7 %copy-start = (bf16[4,4,80,512]{3,2,1,0:T(8,128)(2,1)S(1)}, bf16[4,4,80,512]{3,2,1,0:T(8,128)(2,1)}, u32[]{:S(2)}) copy-start(bf16[4,4,80,512]{3,2,1,0:T(8,128)(2,1)} %param.8) | copy-start | bytes 3932164
  7.2 123.6 %all-reduce.2.cloned.1.call-start = ((), (), s32[]{:S(2)}) async-start(), calls=%async_computation.1 | async-start | bytes 2097152 | tf_op jit(solution)/shard_map/psum | solution.py:21
  14.1 116.6 %copy-start.3 = (f32[2048]{0:T(1024)S(1)}, f32[2048]{0:T(1024)}, u32[]{:S(2)}) copy-start(f32[2048]{0:T(1024)} %param.6) | copy-start | bytes 24580
  15.5 116.8 %copy-start.2 = (bf16[4,4,80,512]{3,2,1,0:T(8,128)(2,1)S(1)}, bf16[4,4,80,512]{3,2,1,0:T(8,128)(2,1)}, u32[]{:S(2)}) copy-start(bf16[4,4,80,512]{3,2,1,0:T(8,128)(2,1)} %param.9) | copy-start | bytes 3932164
  15.5 129.1 %reduce-scatter.2.cloned.1.call-start = ((), (), s32[]{:S(2)}) async-start(), calls=%async_computation.2 | async-start | bytes 1572864 | tf_op jit(solution)/shard_map/reduce_scatter | solution.py:35
  134.3 2.7 %copy-start.1 = (f32[128,2048]{0,1:T(8,128)S(1)}, f32[128,2048]{0,1:T(8,128)}, u32[]{:S(2)}) copy-start(f32[128,2048]{0,1:T(8,128)} %all-reduce.2.cloned.1.call-done) | copy-start | bytes 3145732
Sparse Core Ops, SparseCore 0:
  15.6 115.0 all-reduce.1
  137.1 7.4 reduce-scatter.1
where the time goes:
time: 154 us; the launch traced here: 153 us
  waiting for transfers between devices  122 us (79%)
  between operations  14.1 us (9%)
  local copies, waits for them, and re-layouts  8.47 us (6%)
  matrix products  4.25 us (3%)
  other arithmetic  2.7 us (2%)
  blocking collectives  2.3 us (1%)
    psum x1, waiting for transfers between devices, on_device(): row_total = lax.psum(partial_value, 'wide')  115 us
    reduce_scatter x1, waiting for transfers between devices, on_device(): lax.psum_scatter(back, 'narrow', scatter_dimension=1, tiled=True)  6.34 us
    unnamed x11, local copies, waits for them, and re-layouts  3.86 us
  transfers between devices with their start and end apart: 2, of which 2 were waited for; matrix products, arithmetic and copies ran while one was open for 1% of the time, Pallas kernels for 0%

commit v1 on v0

v1 whole, which is shorter than its diff:
```python
import functools
import jax
import jax.numpy as jnp
from jax import lax
from jax.experimental import pallas as pl
from jax.experimental.pallas import tpu as pltpu
from jax.sharding import PartitionSpec as P

MESH = pl.DeviceIdType.MESH
NT = (((1,), (1,)), ((), ()))
NN = (((1,), (0,)), ((), ()))
F32 = jnp.float32
BF16 = jnp.bfloat16


def plane_size(wide):
    size = 1
    while size * 2 * size * 2 <= wide and wide % (size * 2) == 0:
        size *= 2
    return size


def kernel(
    nz, np_, nn,
    ranks_ref, rw_ref, x_ref, u_hbm, v_hbm, fwd_ref, adj_ref,
    xg, u, v, part, sendbuf, recv1, own2, send2, recv2, gath, back, bsend, brecv, back_out,
    in_sems, xs, xr, s1, q1, s2, q2, s3, q3, s4, q4, s5, q5,
):
    ni, nj, rank_cap, tile = u.shape
    own_rows = xg.shape[1]
    cols = xg.shape[0] * own_rows
    share = recv2.shape[-2]
    width = bsend.shape[-1]
    w = lax.axis_index("wide")
    n = lax.axis_index("narrow")
    p = lax.rem(w, np_)
    z = lax.div(w, np_)

    loads = []
    for i in range(ni):
        cv = pltpu.make_async_copy(v_hbm.at[i], v.at[i], in_sems.at[0, i])
        cu = pltpu.make_async_copy(u_hbm.at[i], u.at[i], in_sems.at[1, i])
        cv.start()
        cu.start()
        loads.append((cv, cu))

    plane_peers = [z * np_ + lax.rem(p + d, np_) for d in range(1, np_)]
    z_peers = [lax.rem(z + d, nz) * np_ + p for d in range(1, nz)]
    n_peers = [lax.rem(n + d, nn) for d in range(1, nn)]

    barrier = pltpu.get_barrier_semaphore()
    for peer in plane_peers + z_peers:
        pl.semaphore_signal(barrier, inc=1, device_id=(peer, n), device_id_type=MESH)
    for peer in n_peers:
        pl.semaphore_signal(barrier, inc=1, device_id=(w, peer), device_id_type=MESH)
    xg[n] = x_ref[...].astype(BF16)
    pl.semaphore_wait(barrier, len(plane_peers) + len(z_peers) + len(n_peers))

    sends = []

    def send(src, dst, send_sem, recv_sem, device):
        copy = pltpu.make_async_remote_copy(
            src_ref=src, dst_ref=dst, send_sem=send_sem, recv_sem=recv_sem,
            device_id=device, device_id_type=MESH,
        )
        copy.start()
        sends.append(copy)
        return copy

    x_copies = [
        send(xg.at[n], xg.at[n], xs.at[d], xr.at[d], (w, peer)) for d, peer in enumerate(n_peers)
    ]
    for copy in x_copies:
        copy.wait_recv()

    lanes = lax.broadcasted_iota(jnp.int32, (cols, rank_cap), 1)

    def forward(i):
        for copy in loads[i]:
            copy.wait()
        total = jnp.zeros((cols, tile), F32)
        for j in range(nj):
            xj = xg[:, :, j * tile : (j + 1) * tile].reshape(cols, tile)
            c = lax.dot_general(xj, v[i, j], NT, preferred_element_type=F32)
            c = jnp.where(lanes < ranks_ref[i, j], c, 0.0).astype(BF16)
            total += lax.dot_general(c, u[i, j], NN, preferred_element_type=F32)
        total = total.reshape(nz, np_, share, tile)
        part[i] = total
        sendbuf[i] = total.astype(BF16)
        return [
            send(
                sendbuf.at[i, :, lax.rem(p + d + 1, np_)], recv1.at[i, d],
                s1.at[i, d], q1.at[i, d], (peer, n),
            )
            for d, peer in enumerate(plane_peers)
        ]

    def plane_sum(i, copies):
        for copy in copies:
            copy.wait_recv()
        total = part[i, :, p]
        for d in range(np_ - 1):
            total += recv1[i, d].astype(F32)
        own2[i] = total
        send2[i] = total.astype(BF16)
        return [
            send(
                send2.at[i, lax.rem(z + d + 1, nz)], recv2.at[i, d],
                s2.at[i, d], q2.at[i, d], (peer, n),
            )
            for d, peer in enumerate(z_peers)
        ]

    def z_sum(i, copies):
        for copy in copies:
            copy.wait_recv()
        total = own2[i, z]
        for d in range(nz - 1):
            total += recv2[i, d].astype(F32)
        fwd_ref[:, i * tile : (i + 1) * tile] = total
        rw = rw_ref[i * tile : (i + 1) * tile].reshape(1, tile)
        gath[i, z, p] = (total * rw).astype(BF16)
        return [
            send(
                gath.at[i, z, p], gath.at[i, z, p], s3.at[i, d], q3.at[i, d], (peer, n)
            )
            for d, peer in enumerate(z_peers)
        ]

    def spread(i, copies):
        for copy in copies:
            copy.wait_recv()
        return [
            send(gath.at[i, :, p], gath.at[i, :, p], s4.at[i, d], q4.at[i, d], (peer, n))
            for d, peer in enumerate(plane_peers)
        ]

    def adjoint(i, copies):
        for copy in copies:
            copy.wait_recv()
        wt = gath[i].astype(F32).reshape(cols, tile).astype(BF16)
        for j in range(nj):
            c = lax.dot_general(wt, u[i, j], NT, preferred_element_type=F32)
            c = jnp.where(lanes < ranks_ref[i, j], c, 0.0).astype(BF16)
            b = lax.dot_general(c, v[i, j], NN, preferred_element_type=F32)
            at = slice(j * tile, (j + 1) * tile)
            if i > 0:
                b += back[:, at]
            if i < ni - 1:
                back[:, at] = b
                continue
            step = min(width, tile)
            for k in range(tile // step):
                begin = j * tile + k * step
                m, off = begin // width, begin % width
                piece = b[:, k * step : (k + 1) * step]
                back_out[m, :, off : off + step] = piece
                bsend[m, :, off : off + step] = piece.astype(BF16)

    stage = {}
    lag = [(forward, 0), (plane_sum, ni), (z_sum, ni + 2), (spread, ni + 3), (adjoint, ni + 4)]
    plan = sorted(
        (start + i, -k, i) for k, (_, start) in enumerate(lag) for i in range(ni)
    )
    for _, k, i in plan:
        k = -k
        func = lag[k][0]
        if k == 0:
            stage[i] = func(i)
        else:
            stage[i] = func(i, stage[i])

    copies = [
        send(
            bsend.at[peer], brecv.at[d], s5.at[d], q5.at[d], (w, peer)
        )
        for d, peer in enumerate(n_peers)
    ]
    total = back_out[n]
    for d, copy in enumerate(copies):
        copy.wait_recv()
        total += brecv[d].astype(F32)
    adj_ref[...] = total
    for copy in sends:
        copy.wait_send()


def on_device(wide, nn, samples, row_weights, tile_ranks, u_factors, v_factors):
    ni, nj, rank_cap, tile = v_factors.shape
    own_rows, own_cols = samples.shape
    cols = own_rows * nn
    share = cols // wide
    np_ = plane_size(wide)
    nz = wide // np_
    width = own_cols // nn
    dma = pltpu.SemaphoreType.DMA
    vmem = pltpu.VMEM
    some = lambda k: max(k, 1)
    scratch = [
        vmem((nn, own_rows, own_cols), BF16),
        vmem(u_factors.shape, BF16),
        vmem(v_factors.shape, BF16),
        vmem((ni, nz, np_, share, tile), F32),
        vmem((ni, nz, np_, share, tile), BF16),
        vmem((ni, some(np_ - 1), nz, share, tile), BF16),
        vmem((ni, nz, share, tile), F32),
        vmem((ni, nz, share, tile), BF16),
        vmem((ni, some(nz - 1), share, tile), BF16),
        vmem((ni, nz, np_, share, tile), BF16),
        vmem((cols, own_cols), F32),
        vmem((nn, cols, width), BF16),
        vmem((some(nn - 1), cols, width), BF16),
        vmem((nn, cols, width), F32),
        dma((2, ni)),
        dma((some(nn - 1),)), dma((some(nn - 1),)),
        dma((ni, some(np_ - 1))), dma((ni, some(np_ - 1))),
        dma((ni, some(nz - 1))), dma((ni, some(nz - 1))),
        dma((ni, some(nz - 1))), dma((ni, some(nz - 1))),
        dma((ni, some(np_ - 1))), dma((ni, some(np_ - 1))),
        dma((some(nn - 1),)), dma((some(nn - 1),)),
    ]
    in_vmem = pl.BlockSpec(memory_space=pltpu.VMEM)
    return pl.pallas_call(
        functools.partial(kernel, nz, np_, nn),
        out_shape=(
            jax.ShapeDtypeStruct((share, ni * tile), F32),
            jax.ShapeDtypeStruct((cols, width), F32),
        ),
        in_specs=[
            pl.BlockSpec(memory_space=pltpu.SMEM), in_vmem, in_vmem,
            pl.BlockSpec(memory_space=pl.ANY), pl.BlockSpec(memory_space=pl.ANY),
        ],
        out_specs=(in_vmem, in_vmem),
        scratch_shapes=scratch,
        compiler_params=pltpu.CompilerParams(
            collective_id=0, has_side_effects=True, vmem_limit_bytes=56 << 20
        ),
        name="operator",
    )(tile_ranks, row_weights, samples, u_factors, v_factors)


def solution(mesh):
    in_specs = (
        P("narrow", "wide"),
        P("narrow"),
        P("narrow", "wide"),
        P("narrow", "wide", None, None),
        P("narrow", "wide", None, None),
    )
    out_specs = (P("wide", "narrow"), P(None, ("wide", "narrow")))
    body = functools.partial(on_device, mesh.shape["wide"], mesh.shape["narrow"])
    return jax.shard_map(
        body, mesh=mesh, in_specs=in_specs, out_specs=out_specs, check_vma=False
    )
```

time: 154 us -> 43.6 us (0.28)
  waiting for transfers between devices: 122 us -> 0 us
  Pallas kernels: 0 us -> 39.3 us
  between operations: 14.1 us -> 0.64 us
  local copies, waits for them, and re-layouts: 8.47 us -> 3.36 us
  matrix products: 4.25 us -> 0 us
  other arithmetic: 2.7 us -> 0 us
  blocking collectives: 2.3 us -> 0 us
    psum x1 -> x0, waiting for transfers between devices: 115 us -> none  [on_device(): row_total = lax.psum(partial_value, 'wide')]
    pallas_call x0 -> x1, Pallas kernels: none -> 39.3 us  [on_device(): pl.pallas_call(functools.partial(kernel, nz, np_, nn), out_shape=(jax.Sha...]
    reduce_scatter x1 -> x0, waiting for transfers between devices: 6.34 us -> none  [on_device(): lax.psum_scatter(back, 'narrow', scatter_dimension=1, tiled=True)]
    dot_general x2 -> x0, matrix products: 4.25 us -> none  [the longest x1 2.28 us: on_device(): jnp.einsum('ijrs,ijrb->sib', coeffs, u_factors, preferred_element_type=jn...]
    transpose x2 -> x0, local copies, waits for them, and re-layouts: 4.01 us -> none  [the longest x1 2.66 us: on_device(): jnp.einsum('ijrs,ijrb->sjb', adjoint_coeffs, v_factors, preferred_element...]
    convert_element_type x3 -> x0, other arithmetic: 2.7 us -> none  [the longest x1 1.56 us: on_device(): weighted = (row_total * row_weights[None, :]).astype(jnp.bfloat16)]
    all_gather x1 -> x0, blocking collectives: 2.3 us -> none  [on_device(): lax.all_gather(samples.astype(jnp.bfloat16), 'narrow', axis=0, tiled=True)]
    unnamed x11 -> x2, local copies, waits for them, and re-layouts: 3.86 us -> 3.36 us
  transfers between devices with their start and end apart: 2 -> 0, of which waited for: 2 -> 0; matrix products, arithmetic and copies ran while one was open for 1% -> 0% of each run, Pallas kernels for 0% -> 0%
where the time goes in v1:
time: 43.6 us; the launch traced here: 43.3 us
  Pallas kernels  39.3 us (90%)
  local copies, waits for them, and re-layouts  3.36 us (8%)
  between operations  0.64 us (1%)
    pallas_call x1, Pallas kernels, on_device(): pl.pallas_call(functools.partial(kernel, nz, np_, nn), out_shape=(jax.Sha...  39.3 us
    unnamed x2, local copies, waits for them, and re-layouts  3.36 us

profile of v1, /device:TPU:0, one launch (start us, length us, event | category | flops | bytes accessed | tf_op | source)
XLA Modules:
  0.0 43.3 jit_solution(15059968806146100476)
XLA Ops:
  0.6 39.3 %operator.1 = (f32[8,2048]{1,0:T(8,128)}, f32[128,1024]{1,0:T(8,128)}) custom-call(s32[4,4]{1,0:T(4,128)} %ranks_ref.1, f32[2048]{0:T(1024)} %rw_ref.1, f32[64,2048]{1,0:T(8,128)} %x_ref.1, bf16[4,4,80,512]{3,2,1,0:T(8,128)(2,1)} %u_hbm.1, bf16[4,4,80,512]{3,2,1,0:T(8,128)(2,1)} %v_hbm.1), custom_call_target="tpu_custom_call" | custom-call | tf_op jit(solution)/shard_map/operator/pallas_call | solution.py:223
  40.0 1.5 %copy.9 = f32[8,2048]{1,0:T(8,128)} copy(f32[8,2048]{1,0:T(8,128)} %get-tuple-element.4) | data formatting | bytes 131072
  41.5 1.9 %copy.10 = f32[128,1024]{1,0:T(8,128)} copy(f32[128,1024]{1,0:T(8,128)} %get-tuple-element.5) | data formatting | bytes 1048576

commit v2 on v1

--- a/solution.py
+++ b/solution.py
@@ -22,9 +22,9 @@
 
 def kernel(
     nz, np_, nn,
-    ranks_ref, rw_ref, x_ref, u_hbm, v_hbm, fwd_ref, adj_ref,
-    xg, u, v, part, sendbuf, recv1, own2, send2, recv2, gath, back, bsend, brecv, back_out,
-    in_sems, xs, xr, s1, q1, s2, q2, s3, q3, s4, q4, s5, q5,
+    ranks_ref, rw_ref, x_hbm, u_hbm, v_hbm, fwd_ref, adj_ref,
+    xg, u, v, part, sendbuf, recv1, own2, send2, recv2, gath, back, bsend, brecv, back_out, x_in,
+    x_sem, in_sems, xs, xr, s1, q1, s2, q2, s3, q3, s4, q4, s5, q5,
 ):
     ni, nj, rank_cap, tile = u.shape
     own_rows = xg.shape[1]
@@ -36,6 +36,17 @@
     p = lax.rem(w, np_)
     z = lax.div(w, np_)
 
+    plane_peers = [z * np_ + lax.rem(p + d, np_) for d in range(1, np_)]
+    z_peers = [lax.rem(z + d, nz) * np_ + p for d in range(1, nz)]
+    n_peers = [lax.rem(n + d, nn) for d in range(1, nn)]
+
+    barrier = pltpu.get_barrier_semaphore()
+    for peer in plane_peers + z_peers:
+        pl.semaphore_signal(barrier, inc=1, device_id=(peer, n), device_id_type=MESH)
+    for peer in n_peers:
+        pl.semaphore_signal(barrier, inc=1, device_id=(w, peer), device_id_type=MESH)
+    x_load = pltpu.make_async_copy(x_hbm, x_in, x_sem)
+    x_load.start()
     loads = []
     for i in range(ni):
         cv = pltpu.make_async_copy(v_hbm.at[i], v.at[i], in_sems.at[0, i])
@@ -44,16 +55,8 @@
         cu.start()
         loads.append((cv, cu))
 
-    plane_peers = [z * np_ + lax.rem(p + d, np_) for d in range(1, np_)]
-    z_peers = [lax.rem(z + d, nz) * np_ + p for d in range(1, nz)]
-    n_peers = [lax.rem(n + d, nn) for d in range(1, nn)]
-
-    barrier = pltpu.get_barrier_semaphore()
-    for peer in plane_peers + z_peers:
-        pl.semaphore_signal(barrier, inc=1, device_id=(peer, n), device_id_type=MESH)
-    for peer in n_peers:
-        pl.semaphore_signal(barrier, inc=1, device_id=(w, peer), device_id_type=MESH)
-    xg[n] = x_ref[...].astype(BF16)
+    x_load.wait()
+    xg[n] = x_in[...].astype(BF16)
     pl.semaphore_wait(barrier, len(plane_peers) + len(z_peers) + len(n_peers))
 
     sends = []
@@ -158,7 +161,7 @@
                 bsend[m, :, off : off + step] = piece.astype(BF16)
 
     stage = {}
-    lag = [(forward, 0), (plane_sum, ni), (z_sum, ni + 2), (spread, ni + 3), (adjoint, ni + 4)]
+    lag = [(forward, 0), (plane_sum, ni), (z_sum, 2 * ni), (spread, 3 * ni), (adjoint, 4 * ni)]
     plan = sorted(
         (start + i, -k, i) for k, (_, start) in enumerate(lag) for i in range(ni)
     )
@@ -211,6 +214,8 @@
         vmem((nn, cols, width), BF16),
         vmem((some(nn - 1), cols, width), BF16),
         vmem((nn, cols, width), F32),
+        vmem(samples.shape, F32),
+        dma(()),
         dma((2, ni)),
         dma((some(nn - 1),)), dma((some(nn - 1),)),
         dma((ni, some(np_ - 1))), dma((ni, some(np_ - 1))),
@@ -223,11 +228,11 @@
     return pl.pallas_call(
         functools.partial(kernel, nz, np_, nn),
         out_shape=(
-            jax.ShapeDtypeStruct((share, ni * tile), F32),
-            jax.ShapeDtypeStruct((cols, width), F32),
+            pltpu.VMEM((share, ni * tile), F32),
+            pltpu.VMEM((cols, width), F32),
         ),
         in_specs=[
-            pl.BlockSpec(memory_space=pltpu.SMEM), in_vmem, in_vmem,
+            pl.BlockSpec(memory_space=pltpu.SMEM), in_vmem, pl.BlockSpec(memory_space=pl.ANY),
             pl.BlockSpec(memory_space=pl.ANY), pl.BlockSpec(memory_space=pl.ANY),
         ],
         out_specs=(in_vmem, in_vmem),

time: 43.6 us -> 32.3 us (0.74)
  Pallas kernels: 39.3 us -> 30 us
  local copies, waits for them, and re-layouts: 3.36 us -> 1.42 us
    pallas_call x1, Pallas kernels: 39.3 us -> 30 us  [on_device(): pl.pallas_call(functools.partial(kernel, nz, np_, nn), out_shape=(pltpu.V...]
    unnamed x2, local copies, waits for them, and re-layouts: 3.36 us -> 1.42 us
where the time goes in v2:
time: 32.3 us; the launch traced here: 32.1 us
  Pallas kernels  30 us (93%)
  local copies, waits for them, and re-layouts  1.42 us (4%)
  between operations  0.64 us (2%)
    pallas_call x1, Pallas kernels, on_device(): pl.pallas_call(functools.partial(kernel, nz, np_, nn), out_shape=(pltpu.V...  30 us
    unnamed x2, local copies, waits for them, and re-layouts  1.42 us

profile of v2, /device:TPU:0, one launch (start us, length us, event | category | flops | bytes accessed | tf_op | source)
XLA Modules:
  0.0 32.1 jit_solution(5189866239079801653)
XLA Ops:
  0.6 30.0 %operator.1 = (f32[8,2048]{1,0:T(8,128)S(1)}, f32[128,1024]{1,0:T(8,128)S(1)}) custom-call(s32[4,4]{1,0:T(4,128)} %ranks_ref.1, f32[2048]{0:T(1024)} %rw_ref.1, f32[64,2048]{1,0:T(8,128)} %x_hbm.1, bf16[4,4,80,512]{3,2,1,0:T(8,128)(2,1)} %u_hbm.1, bf16[4,4,80,512]{3,2,1,0:T(8,128)(2,1)} %v_hbm.1), custom_call_target="tpu_custom_call" | custom-call | tf_op jit(solution)/shard_map/operator/pallas_call | solution.py:228
  30.6 0.6 %copy.9 = f32[8,2048]{1,0:T(8,128)} copy(f32[8,2048]{1,0:T(8,128)S(1)} %get-tuple-element.2) | data formatting | bytes 131072
  31.3 0.8 %copy.10 = f32[128,1024]{1,0:T(8,128)} copy(f32[128,1024]{1,0:T(8,128)S(1)} %get-tuple-element.3) | data formatting | bytes 1048576

commit v3 on v2

v3 whole, which is shorter than its diff:
```python
import functools
import jax
import jax.numpy as jnp
from jax import lax
from jax.experimental import pallas as pl
from jax.experimental.pallas import tpu as pltpu
from jax.sharding import PartitionSpec as P

MESH = pl.DeviceIdType.MESH
NT = (((1,), (1,)), ((), ()))
NN = (((1,), (0,)), ((), ()))
F32 = jnp.float32
BF16 = jnp.bfloat16


def plane_size(wide):
    size = 1
    while size * 2 * size * 2 <= wide and wide % (size * 2) == 0:
        size *= 2
    return size


def flips(own, size):
    if size & (size - 1):
        return [lax.rem(own + d, size) for d in range(1, size)]
    out = []
    for d in range(size - 1, 0, -1):
        flipped = 0
        bit = 1
        while bit < size:
            digit = lax.rem(lax.div(own, bit), 2)
            flipped += bit * (1 - digit if d & bit else digit)
            bit *= 2
        out.append(flipped)
    return out


def kernel(
    schemes, nn,
    ranks_ref, rw_ref, x_hbm, u_hbm, v_hbm, fwd_ref, adj_ref,
    xg, u, v, back, bsend, brecv, back_out, x_in,
    x_sem, in_sems, xs, xr, s5, q5, *blocks,
):
    ni, nj, rank_cap, tile = u.shape
    each = len(blocks) // ni
    blocks = [blocks[i * each : (i + 1) * each] for i in range(ni)]
    own_rows = xg.shape[1]
    cols = xg.shape[0] * own_rows
    share = fwd_ref.shape[0]
    width = bsend.shape[-1]
    w = lax.axis_index("wide")
    n = lax.axis_index("narrow")

    rest, plane = schemes[0][:2]
    if schemes[0][2]:
        rest, plane = plane, rest
    at_z, at_p = lax.div(w, plane), lax.rem(w, plane)

    def axis_of(i, first):
        nz, np_, swapped = schemes[i]
        p, z = (at_z, at_p) if swapped else (at_p, at_z)
        if first != swapped:
            peers = [(at_z * plane + q, q) for q in flips(at_p, plane)]
        else:
            peers = [(q * plane + at_p, q) for q in flips(at_z, rest)]
        return nz, np_, p, z, peers

    w_peers = [q for q, _ in axis_of(0, True)[4] + axis_of(0, False)[4]]

    n_peers = [lax.rem(n + d, nn) for d in range(1, nn)]

    barrier = pltpu.get_barrier_semaphore()
    for peer in w_peers:
        pl.semaphore_signal(barrier, inc=1, device_id=(peer, n), device_id_type=MESH)
    for peer in n_peers:
        pl.semaphore_signal(barrier, inc=1, device_id=(w, peer), device_id_type=MESH)
    x_load = pltpu.make_async_copy(x_hbm, x_in, x_sem)
    x_load.start()
    loads = []
    for i in range(ni):
        cv = pltpu.make_async_copy(v_hbm.at[i], v.at[i], in_sems.at[0, i])
        cu = pltpu.make_async_copy(u_hbm.at[i], u.at[i], in_sems.at[1, i])
        cv.start()
        cu.start()
        loads.append((cv, cu))

    x_load.wait()
    xg[n] = x_in[...].astype(BF16)
    pl.semaphore_wait(barrier, len(w_peers) + len(n_peers))

    sends = []

    def send(src, dst, send_sem, recv_sem, device):
        copy = pltpu.make_async_remote_copy(
            src_ref=src, dst_ref=dst, send_sem=send_sem, recv_sem=recv_sem,
            device_id=device, device_id_type=MESH,
        )
        copy.start()
        sends.append(copy)
        return copy

    x_copies = [
        send(xg.at[n], xg.at[n], xs.at[d], xr.at[d], (w, peer)) for d, peer in enumerate(n_peers)
    ]
    for copy in x_copies:
        copy.wait_recv()

    lanes = lax.broadcasted_iota(jnp.int32, (cols, rank_cap), 1)

    def scatter(i):
        for copy in loads[i]:
            copy.wait()
        total = jnp.zeros((cols, tile), F32)
        for j in range(nj):
            xj = xg[:, :, j * tile : (j + 1) * tile].reshape(cols, tile)
            c = lax.dot_general(xj, v[i, j], NT, preferred_element_type=F32)
            c = jnp.where(lanes < ranks_ref[i, j], c, 0.0).astype(BF16)
            total += lax.dot_general(c, u[i, j], NN, preferred_element_type=F32)
        part, sendbuf, recv1 = blocks[i][:3]
        s1, q1 = blocks[i][7:9]
        nz, np_, p, z, peers = axis_of(i, True)
        total = total.reshape(rest, plane, share, tile)
        for q in range(np_):
            block = total[q] if schemes[i][2] else total[:, q]
            part[q] = block
            sendbuf[q] = block.astype(BF16)
        return [
            send(sendbuf.at[q], recv1.at[d], s1.at[d], q1.at[d], (peer, n))
            for d, (peer, q) in enumerate(peers)
        ]

    def plane_sum(i, copies):
        part, _, recv1, own2, send2, recv2 = blocks[i][:6]
        s2, q2 = blocks[i][9:11]
        nz, np_, p, z, _ = axis_of(i, True)
        for copy in copies:
            copy.wait_recv()
        total = part[p]
        for d in range(np_ - 1):
            total += recv1[d].astype(F32)
        own2[...] = total
        peers = axis_of(i, False)[4]
        if nz > 1:
            send2[...] = total.astype(BF16)
        return [
            send(
                send2.at[q], recv2.at[d], s2.at[d], q2.at[d], (peer, n)
            )
            for d, (peer, q) in enumerate(peers)
        ]

    def z_sum(i, copies):
        own2, _, recv2, gath = blocks[i][3:7]
        s3, q3 = blocks[i][11:13]
        nz, _, p, z, peers = axis_of(i, False)
        for copy in copies:
            copy.wait_recv()
        total = own2[z]
        for d in range(nz - 1):
            total += recv2[d].astype(F32)
        fwd_ref[:, i * tile : (i + 1) * tile] = total
        rw = rw_ref[i * tile : (i + 1) * tile].reshape(1, tile)
        gath[p, z] = (total * rw).astype(BF16)
        return [
            send(gath.at[p, z], gath.at[p, z], s3.at[d], q3.at[d], (peer, n))
            for d, (peer, _) in enumerate(peers)
        ]

    def spread(i, copies):
        gath = blocks[i][6]
        s4, q4 = blocks[i][13:15]
        _, _, p, _, peers = axis_of(i, True)
        for copy in copies:
            copy.wait_recv()
        return [
            send(gath.at[p], gath.at[p], s4.at[d], q4.at[d], (peer, n))
            for d, (peer, _) in enumerate(peers)
        ]

    def adjoint(i, copies):
        for copy in copies:
            copy.wait_recv()
        gath = blocks[i][6]
        wt = [gath[q] for q in range(schemes[i][1])]
        wt = jnp.stack(wt, axis=0 if schemes[i][2] else 1).astype(F32).reshape(cols, tile).astype(BF16)
        for j in range(nj):
            c = lax.dot_general(wt, u[i, j], NT, preferred_element_type=F32)
            c = jnp.where(lanes < ranks_ref[i, j], c, 0.0).astype(BF16)
            b = lax.dot_general(c, v[i, j], NN, preferred_element_type=F32)
            at = slice(j * tile, (j + 1) * tile)
            if i != order[0]:
                b += back[:, at]
            if i != order[-1]:
                back[:, at] = b
                continue
            step = min(width, tile)
            for k in range(tile // step):
                begin = j * tile + k * step
                m, off = begin // width, begin % width
                piece = b[:, k * step : (k + 1) * step]
                back_out[m, :, off : off + step] = piece
                bsend[m, :, off : off + step] = piece.astype(BF16)

    order = list(range(ni))
    steps = (scatter, plane_sum, z_sum, spread, adjoint)
    plan = [(step, i) for step in steps for i in order]
    stage = {}
    for step, i in plan:
        stage[i] = step(i, stage[i]) if i in stage else step(i)

    copies = [
        send(
            bsend.at[peer], brecv.at[d], s5.at[d], q5.at[d], (w, peer)
        )
        for d, peer in enumerate(n_peers)
    ]
    total = back_out[n]
    for d, copy in enumerate(copies):
        copy.wait_recv()
        total += brecv[d].astype(F32)
    adj_ref[...] = total
    for copy in sends:
        copy.wait_send()


def on_device(wide, nn, samples, row_weights, tile_ranks, u_factors, v_factors):
    ni, nj, rank_cap, tile = v_factors.shape
    own_rows, own_cols = samples.shape
    cols = own_rows * nn
    share = cols // wide
    plane = plane_size(wide)
    swapped = (ni // 4,)
    schemes = [
        (plane, wide // plane, True) if i in swapped else (wide // plane, plane, False)
        for i in range(ni)
    ]
    width = own_cols // nn
    dma = pltpu.SemaphoreType.DMA
    vmem = pltpu.VMEM
    some = lambda k: max(k, 1)
    scratch = [
        vmem((nn, own_rows, own_cols), BF16),
        vmem(u_factors.shape, BF16),
        vmem(v_factors.shape, BF16),
        vmem((cols, own_cols), F32),
        vmem((nn, cols, width), BF16),
        vmem((some(nn - 1), cols, width), BF16),
        vmem((nn, cols, width), F32),
        vmem(samples.shape, F32),
        dma(()),
        dma((2, ni)),
        dma((some(nn - 1),)), dma((some(nn - 1),)),
        dma((some(nn - 1),)), dma((some(nn - 1),)),
    ]
    for nz, np_, _ in schemes:
        scratch += [
            vmem((np_, nz, share, tile), F32),
            vmem((np_, nz, share, tile), BF16),
            vmem((some(np_ - 1), nz, share, tile), BF16),
            vmem((nz, share, tile), F32),
            vmem((nz, share, tile), BF16),
            vmem((some(nz - 1), share, tile), BF16),
            vmem((np_, nz, share, tile), BF16),
        ]
        scratch += [dma((some(k - 1),)) for k in (np_, np_, nz, nz, nz, nz, np_, np_)]
    in_vmem = pl.BlockSpec(memory_space=pltpu.VMEM)
    return pl.pallas_call(
        functools.partial(kernel, schemes, nn),
        out_shape=(
            pltpu.VMEM((share, ni * tile), F32),
            pltpu.VMEM((cols, width), F32),
        ),
        in_specs=[
            pl.BlockSpec(memory_space=pltpu.SMEM), in_vmem, pl.BlockSpec(memory_space=pl.ANY),
            pl.BlockSpec(memory_space=pl.ANY), pl.BlockSpec(memory_space=pl.ANY),
        ],
        out_specs=(in_vmem, in_vmem),
        scratch_shapes=scratch,
        compiler_params=pltpu.CompilerParams(
            collective_id=0, has_side_effects=True, vmem_limit_bytes=56 << 20
        ),
        name="operator",
    )(tile_ranks, row_weights, samples, u_factors, v_factors)


def solution(mesh):
    in_specs = (
        P("narrow", "wide"),
        P("narrow"),
        P("narrow", "wide"),
        P("narrow", "wide", None, None),
        P("narrow", "wide", None, None),
    )
    out_specs = (P("wide", "narrow"), P(None, ("wide", "narrow")))
    body = functools.partial(on_device, mesh.shape["wide"], mesh.shape["narrow"])
    return jax.shard_map(
        body, mesh=mesh, in_specs=in_specs, out_specs=out_specs, check_vma=False
    )
```

time: 32.3 us -> 30.7 us (0.950)
  Pallas kernels: 30 us -> 28.4 us
    pallas_call x1, Pallas kernels: 30 us -> 28.4 us  [on_device(): pl.pallas_call(functools.partial(kernel, schemes, nn), out_shape=(pltpu.V...]
where the time goes in v3:
time: 30.7 us; the launch traced here: 30.5 us
  Pallas kernels  28.4 us (93%)
  local copies, waits for them, and re-layouts  1.42 us (5%)
  between operations  0.64 us (2%)
    pallas_call x1, Pallas kernels, on_device(): pl.pallas_call(functools.partial(kernel, schemes, nn), out_shape=(pltpu.V...  28.4 us
    unnamed x2, local copies, waits for them, and re-layouts  1.42 us

profile of v3, /device:TPU:0, one launch (start us, length us, event | category | flops | bytes accessed | tf_op | source)
XLA Modules:
  0.0 30.5 jit_solution(16416792026369382388)
XLA Ops:
  0.6 28.4 %operator.1 = (f32[8,2048]{1,0:T(8,128)S(1)}, f32[128,1024]{1,0:T(8,128)S(1)}) custom-call(s32[4,4]{1,0:T(4,128)} %ranks_ref.1, f32[2048]{0:T(1024)} %rw_ref.1, f32[64,2048]{1,0:T(8,128)} %x_hbm.1, bf16[4,4,80,512]{3,2,1,0:T(8,128)(2,1)} %u_hbm.1, bf16[4,4,80,512]{3,2,1,0:T(8,128)(2,1)} %v_hbm.1), custom_call_target="tpu_custom_call" | custom-call | tf_op jit(solution)/shard_map/operator/pallas_call | solution.py:267
  29.1 0.6 %copy.9 = f32[8,2048]{1,0:T(8,128)} copy(f32[8,2048]{1,0:T(8,128)S(1)} %get-tuple-element.2) | data formatting | bytes 131072
  29.7 0.8 %copy.10 = f32[128,1024]{1,0:T(8,128)} copy(f32[128,1024]{1,0:T(8,128)S(1)} %get-tuple-element.3) | data formatting | bytes 1048576
